TPU v7x, 128 devices: a whole 4x4x4 slice. The times are simulated.
128 devices in a mesh: dp: 16 (over x_lo, z, core), loop: 8 (over x_hi, y).
Axes of the slice: x: 4 (x_hi: 2, x_lo: 2; x = x_hi * 2 + x_lo), y: 4, z: 4, core: 2. Of those that a mesh axis runs over, the one named last changes fastest.
Arguments:
- crop_tokens: bfloat16 [8192, 64, 1152], P(('dp', 'loop')), may hold values from -6 to 6
- crop_lengths: int32 [128, 64], P(('dp', 'loop')), may hold values from 1 to 64, 3072 in all within a row
- crop_owner: int32 [8192, 1], P(('dp', 'loop')), may hold values from 0 to 15; in each aligned block of 64 rows (0 to 63, 64 to 127, ...) at most 8 rows name the same one
- crop_slot: int32 [8192], P(('dp', 'loop')), may hold values from 0 to 31
- base_tokens: bfloat16 [4096, 32, 1152], P(('dp', 'loop')), may hold values from -1024 to 1024
- key_probe: bfloat16 [1152, 16], replicated, may hold values from -1 to 1
- value_weight: bfloat16 [1152, 1152], replicated, may hold values from -0.1875 to 0.1875
- out_weight: bfloat16 [1152, 1152], replicated, may hold values from -0.1875 to 0.1875
- text_embed: bfloat16 [4096, 1152], P(('dp', 'loop')), may hold values from -6 to 6
- pair_labels: int32 [4096], P(('dp', 'loop')), may hold values from 0 to 63
- logit_scale: float32 [1], replicated, may hold values from 2 to 8
- logit_bias: float32 [1], replicated, may hold values from -4 to -1
Outputs:
- image_embed: bfloat16 [4096, 1152], P(('dp', 'loop'))
- image_grad: float32 [4096, 1152], P(('dp', 'loop'))
- text_grad: float32 [4096, 1152], P(('dp', 'loop'))
Inputs may be any that keep to these rules, and one draw needn't show every extreme that they name: `crop_owner`: at most 8 of the crops of one device name the same owner, and in every draw the crops of some device name one owner exactly 8 times. `crop_lengths`: the lengths of one device's crops sum to 3072 and the longest is exactly 64.
All inputs are finite; a program needn't handle non-finite values.
Results may differ from a plain program's by a relative error of at most 0.01.
Values may be sent and summed in bfloat16 or wider, within the bound.
No kernel may reach another device: no remote copies, remote signals or barrier semaphores. Data moves between devices by JAX's collectives and lax.ppermute only.
A program may use at most 192 MiB of HBM per device.

v0:
```python
import math
import jax
import jax.numpy as jnp
from jax import lax
from jax.sharding import PartitionSpec as P

very_low = -1e30
norm_eps = 1e-06
highest = lax.Precision.HIGHEST


def crop_partial(tokens, lengths, key_probe, value_weight):
    lead_shape = tokens.shape[:-2]
    crop_width = tokens.shape[-2]
    model_width = tokens.shape[-1]
    head_count = key_probe.shape[1]
    head_dim = model_width // head_count
    flat_rows = tokens.reshape(-1, model_width)
    scores = jnp.dot(flat_rows, key_probe, preferred_element_type=jnp.float32) / math.sqrt(head_dim)
    scores = scores.reshape(lead_shape + (crop_width, head_count))
    position = lax.broadcasted_iota(jnp.int32, lead_shape + (crop_width,), len(lead_shape))
    is_valid = (position < lengths[..., None])[..., None]
    masked = jnp.where(is_valid, scores, very_low)
    maxima = jnp.max(masked, axis=-2)
    weight = jnp.where(is_valid, jnp.exp(masked - maxima[..., None, :]), 0.0)
    totals = jnp.sum(weight, axis=-2)
    mixed = jnp.einsum("...kh,...kd->...hd", weight, tokens.astype(jnp.float32), precision=highest)
    value_heads = value_weight.astype(jnp.float32).reshape(model_width, head_count, head_dim)
    projected = jnp.einsum("...hd,dhe->...he", mixed, value_heads, precision=highest)
    return (projected.reshape(lead_shape + (model_width,)), maxima, totals)


def merge_parts(base_parts, arrived_parts, img_count):
    base_sum, base_max, base_total = base_parts
    mixed_sum, maxima, totals, slot_ids = arrived_parts
    slot_count, model_width = mixed_sum.shape
    head_count = maxima.shape[1]
    member = slot_ids[:, None] == lax.broadcasted_iota(jnp.int32, (1, img_count), 1)
    candidates = jnp.where(member[:, :, None], maxima[:, None, :], very_low)
    joint_max = jnp.maximum(base_max, jnp.max(candidates, axis=0))
    member_float = member.astype(jnp.float32)
    joint_at = jnp.dot(member_float, joint_max, precision=highest)
    rescale = jnp.exp(maxima - joint_at)
    base_rescale = jnp.exp(base_max - joint_max)
    scaled = (mixed_sum.reshape(slot_count, head_count, -1) * rescale[:, :, None]).reshape(
        slot_count, model_width
    )
    base_scaled = base_sum.reshape(img_count, head_count, -1) * base_rescale[:, :, None]
    collected = lax.dot_general(member_float, scaled, (((0,), (0,)), ((), ())), precision=highest)
    collected_total = lax.dot_general(
        member_float, totals * rescale, (((0,), (0,)), ((), ())), precision=highest
    )
    denominator = base_total * base_rescale + collected_total
    pooled = (base_scaled + collected.reshape(img_count, head_count, -1)) / denominator[:, :, None]
    return pooled.reshape(img_count, model_width).astype(jnp.bfloat16)


def unit_rows(matrix):
    return (matrix * lax.rsqrt(jnp.sum(matrix * matrix, axis=1, keepdims=True) + norm_eps)).astype(
        jnp.bfloat16
    )


def make_tile(image_rows, text_rows, row_labels, column_labels, scale_value, bias_value):
    logits = (
        scale_value
        * jnp.einsum("id,jd->ij", image_rows, text_rows, preferred_element_type=jnp.float32)
        + bias_value
    )
    target_sign = jnp.where(row_labels[:, None] == column_labels[None, :], 1.0, -1.0)
    return (scale_value * (-target_sign * jax.nn.sigmoid(-target_sign * logits))).astype(
        jnp.bfloat16
    )


def tile_terms(image_unit, text_block, block_labels, own_labels, scale_value, bias_value):
    grad_tile = make_tile(image_unit, text_block, own_labels, block_labels, scale_value, bias_value)
    image_term = jnp.dot(grad_tile, text_block, preferred_element_type=jnp.float32)
    text_term = jnp.einsum("ij,id->jd", grad_tile, image_unit, preferred_element_type=jnp.float32)
    return (image_term, text_term)


def per_device(
    crop_tokens,
    crop_lengths,
    crop_owner,
    crop_slot,
    base_tokens,
    key_probe,
    value_weight,
    out_weight,
    text_embed,
    pair_labels,
    logit_scale,
    logit_bias,
):
    owners = lax.axis_size("dp")
    crop_total = crop_tokens.shape[0]
    crop_width = crop_tokens.shape[1]
    model_width = crop_tokens.shape[2]
    img_count = base_tokens.shape[0]
    capacity = max(2, (2 * crop_total + owners - 1) // owners)
    slot_count = owners * capacity
    lengths = crop_lengths.reshape(-1)
    owner_ids = crop_owner[:, 0]
    member = (owner_ids[:, None] == lax.broadcasted_iota(jnp.int32, (1, owners), 1)).astype(
        jnp.int32
    )
    running = jnp.cumsum(member, axis=0)
    send_rank = jnp.sum(member * running, axis=1) - 1
    send_index = owner_ids * capacity + send_rank
    slot_ids = (
        jnp.zeros((slot_count,), jnp.int32).at[send_index].set(crop_slot).reshape(owners, capacity)
    )
    send_tokens = (
        jnp.zeros((slot_count, crop_width, model_width), jnp.bfloat16)
        .at[send_index]
        .set(crop_tokens)
    )
    send_lengths = jnp.zeros((slot_count,), jnp.int32).at[send_index].set(lengths)
    arrived_tokens = lax.all_to_all(
        send_tokens.reshape(owners, capacity, crop_width, model_width),
        "dp",
        split_axis=0,
        concat_axis=0,
        tiled=True,
    )
    arrived_lengths = lax.all_to_all(
        send_lengths.reshape(owners, capacity), "dp", split_axis=0, concat_axis=0, tiled=True
    )
    arrived_slots = lax.all_to_all(slot_ids, "dp", split_axis=0, concat_axis=0, tiled=True)
    mixed_sum, maxima, totals = crop_partial(
        arrived_tokens, arrived_lengths, key_probe, value_weight
    )
    received = (mixed_sum, maxima, totals, arrived_slots)
    flat_parts = tuple(
        (
            received_item.reshape((slot_count,) + received_item.shape[2:])
            for received_item in received
        )
    )
    base_lengths = jnp.full((img_count,), base_tokens.shape[1], jnp.int32)
    base_parts = crop_partial(base_tokens, base_lengths, key_probe, value_weight)
    pooled = merge_parts(base_parts, flat_parts, img_count)
    features = jnp.dot(pooled, out_weight, preferred_element_type=jnp.float32)
    image_embed = features.astype(jnp.bfloat16)
    image_unit = unit_rows(features)
    text_unit = unit_rows(text_embed.astype(jnp.float32))
    scale_value = logit_scale[0]
    bias_value = logit_bias[0]
    text_block = lax.all_gather(text_unit, "loop", axis=0, tiled=True)
    block_labels = lax.all_gather(pair_labels, "loop", axis=0, tiled=True)
    image_term, text_term = tile_terms(
        image_unit, text_block, block_labels, pair_labels, scale_value, bias_value
    )
    text_grad = lax.psum_scatter(
        text_term.astype(jnp.bfloat16), "loop", scatter_dimension=0, tiled=True
    ).astype(jnp.float32)
    return (image_embed, image_term, text_grad)


def solution(mesh):
    return jax.shard_map(
        per_device,
        mesh=mesh,
        in_specs=(
            P(("dp", "loop"), None, None),
            P(("dp", "loop"), None),
            P(("dp", "loop"), None),
            P(("dp", "loop")),
            P(("dp", "loop"), None, None),
            P(),
            P(),
            P(),
            P(("dp", "loop"), None),
            P(("dp", "loop")),
            P(),
            P(),
        ),
        out_specs=(P(("dp", "loop"), None), P(("dp", "loop"), None), P(("dp", "loop"), None)),
        check_vma=False,
    )
```

profile of v0, /device:TPU:0, one launch (start us, length us, event | category | flops | bytes accessed | tf_op | source)
XLA Modules:
  0.0 538.3 jit_solution(3503626312159067026)
XLA Ops:
  7.2 0.9 fusion.41
  8.2 0.8 select_reduce_fusion.1
  9.0 0.7 fusion.48
  9.7 0.9 scatter_custom_fusion.1
  10.6 0.7 all_to_all.17
  11.3 6.5 %all-to-all-start.1 = ((s32[16,1,8]{2,1,0:T(1,128)}), s32[16,1,8]{2,1,0:T(1,128)S(1)}, u32[]{:S(2)}, u32[]{:S(2)}) async-start(s32[16,1,8]{2,1,0:T(1,128)} %bitcast.8), calls=%async_computation.1 | async-start | bytes 16384 | tf_op jit(solution)/shard_map/all_to_all | solution.py:128
  17.7 0.9 scatter_custom_fusion
  18.6 0.7 all_to_all.15
  19.3 4.4 all-to-all-done.1
  23.7 3.5 all-to-all-start
  27.2 7.2 %broadcast_in_dim.92 = bf16[128,64,1152]{2,1,0:T(8,128)(2,1)} broadcast(bf16[]{:T(256)} %constant.10.clone.1), dimensions={} | broadcast | bytes 18874370 | tf_op jit(solution)/shard_map/broadcast_in_dim | solution.py:116
  34.4 23.5 %scatter_fusion = bf16[128,64,1152]{2,1,0:T(8,128)(2,1)} fusion(bf16[128,64,1152]{2,1,0:T(8,128)(2,1)} %broadcast_in_dim.92, s32[64]{0:T(128)S(1)} %fusion.48, bf16[64,64,1152]{2,1,0:T(8,128)(2,1)} %param.12), kind=kCustom, calls=%fused_computation.2 | custom fusion | bytes 28311808 | tf_op jit(solution)/shard_map/scatter | solution.py:118
  57.9 5.8 %all-to-all-start.2 = ((bf16[16,8,64,1152]{3,2,1,0:T(8,128)(2,1)}), bf16[16,8,64,1152]{3,2,1,0:T(8,128)(2,1)}, u32[]{:S(2)}, u32[]{:S(2)}) async-start(bf16[16,8,64,1152]{3,2,1,0:T(8,128)(2,1)} %bitcast.60), calls=%async_computation.2 | async-start | bytes 37748736 | tf_op jit(solution)/shard_map/all_to_all | solution.py:121
  63.8 2.4 convolution_multiply_fusion.1
  66.3 0.3 fusion.32
  66.6 0.2 copy-done.5
  66.8 0.3 fusion.33
  67.2 5.3 copy.67
  73.8 0.6 dynamic-slice
  75.1 0.2 dynamic-update-slice
  75.3 285.2 %all-reduce = s32[256]{0:T(256)} all-reduce(s32[256]{0:T(256)S(1)} %dynamic-update-slice), channel_id=1, replica_groups=mesh['dp'=16,'loop'=8] {'loop'}, use_global_device_ids=true, to_apply=%add | all-reduce | flops 256 | bytes 2048
  360.7 35.4 %all_gather.7 = bf16[256,1152]{1,0:T(8,128)(2,1)S(1)} all-gather(bf16[32,1152]{1,0:T(8,128)(2,1)S(1)} %fusion.36), channel_id=1, replica_groups=mesh['dp'=16,'loop'=8] {'loop'}, dimensions={0}, use_global_device_ids=true | all-gather | bytes 663552 | tf_op jit(solution)/shard_map/all_gather | solution.py:151
  396.1 4.4 fusion.34
  400.6 0.5 broadcast.92
  401.1 0.7 reduce.3
  401.9 12.1 %convolution_multiply_fusion = f32[8192,16]{0,1:T(8,128)} fusion(bf16[8192,1152]{1,0:T(8,128)(2,1)} %bitcast.11, bf16[1152,16]{0,1:T(8,128)(2,1)} %param.17), kind=kOutput, calls=%fused_computation.5 | convolution fusion | flops 302120960 | bytes 19435520 | tf_op jit(solution)/shard_map/dot_general | solution.py:19
  414.1 2.4 reshape.119
  416.5 2.0 fusion.25
  418.6 0.2 select_reduce_fusion
  418.8 0.1 fusion.24
  419.0 2.4 fusion.26
  421.4 0.9 mul.78
  422.3 2.1 copy.81
  424.4 12.4 %fusion.27 = f32[16,8,16,1152]{3,2,1,0:T(8,128)S(1)} fusion(bf16[16,8,64,1152]{3,2,1,0:T(8,128)(2,1)} %all-to-all-done.2, f32[16,8,64,16]{2,1,0,3:T(8,128)} %reshape.119, f32[16,8,16]{2,1,0:T(8,128)S(1)} %fusion.25, pred[16,8,64]{2,1,0:T(8,128)(4,1)S(1)} %iota_compare_fusion), kind=kOutput, calls=%fused_computation.33 | convolution fusion | flops 1812332544 | bytes 28852224 | tf_op jit(solution)/shard_map/...kh,...kd->...hd/dot_general | solution.py:27
  436.9 7.0 %fusion.4 = f32[16,8,16,72]{3,1,0,2:T(8,128)S(1)} fusion(bf16[1152,16,72,1]{0,2,3,1:T(8,128)(2,1)S(1)} %bitcast.62, f32[16,8,16,1152]{3,2,1,0:T(8,128)S(1)} %fusion.27), kind=kOutput, calls=%fused_computation.9 | convolution fusion | flops 2038431744 | bytes 12681216 | tf_op jit(solution)/shard_map/...hd,dhe->...he/dot_general | solution.py:29
  443.9 1.6 copy.79
  445.5 2.4 reshape_reshape_reshape.3
  447.9 2.1 multiply_bitcast_fusion
  450.0 2.1 copy.82
  452.2 5.3 fusion.10
  457.6 0.9 fusion.14
  458.5 0.2 convert_element_type.37
  458.7 1.3 multiply_reduce_fusion
  460.0 0.3 fusion.23
  460.4 1.2 convolution_convert_fusion
  461.6 0.9 fusion.57
  462.4 67.5 %reduce-scatter.2.cloned.1.call-done = bf16[32,1152]{1,0:T(8,128)(2,1)} async-done(((bf16[256,1152]{1,0:T(8,128)(2,1)}), bf16[32,1152]{1,0:T(8,128)(2,1)}) %reduce-scatter.2.cloned.1.call-update) | async-done | bytes 73744 | tf_op jit(solution)/shard_map/reduce_scatter | solution.py:156
  529.9 1.6 convert_element_type.44
  (42 shorter events, 1.2 us)
Async XLA Ops:
  7.2 451.5 %copy-start = (bf16[1152,1152]{1,0:T(8,128)(2,1)S(1)}, bf16[1152,1152]{1,0:T(8,128)(2,1)}, u32[]{:S(2)}) copy-start(bf16[1152,1152]{1,0:T(8,128)(2,1)} %param.19) | copy-start | bytes 7962628
  11.3 12.5 %all-to-all-start.1 = ((s32[16,1,8]{2,1,0:T(1,128)}), s32[16,1,8]{2,1,0:T(1,128)S(1)}, u32[]{:S(2)}, u32[]{:S(2)}) async-start(s32[16,1,8]{2,1,0:T(1,128)} %bitcast.8), calls=%async_computation.1 | async-start | bytes 16384 | tf_op jit(solution)/shard_map/all_to_all | solution.py:128
  23.7 34.1 %all-to-all-start = ((s32[16,1,8]{2,1,0:T(1,128)}), s32[16,1,8]{2,1,0:T(1,128)S(1)}, u32[]{:S(2)}, u32[]{:S(2)}) async-start(s32[16,1,8]{2,1,0:T(1,128)} %bitcast.6), calls=%async_computation | async-start | bytes 16384 | tf_op jit(solution)/shard_map/all_to_all | solution.py:131
  57.9 5.9 %copy-start.4 = (bf16[1152,16]{0,1:T(8,128)(2,1)S(1)}, bf16[1152,16]{0,1:T(8,128)(2,1)}, u32[]{:S(2)}) copy-start(bf16[1152,16]{0,1:T(8,128)(2,1)} %param.17) | copy-start | bytes 110596
  57.9 344.1 %all-to-all-start.2 = ((bf16[16,8,64,1152]{3,2,1,0:T(8,128)(2,1)}), bf16[16,8,64,1152]{3,2,1,0:T(8,128)(2,1)}, u32[]{:S(2)}, u32[]{:S(2)}) async-start(bf16[16,8,64,1152]{3,2,1,0:T(8,128)(2,1)} %bitcast.60), calls=%async_computation.2 | async-start | bytes 37748736 | tf_op jit(solution)/shard_map/all_to_all | solution.py:121
  63.7 466.2 %reduce-scatter.2.cloned.1.call-start = ((), (), s32[]{:S(2)}) async-start(), calls=%async_computation.4 | async-start | bytes 663552 | tf_op jit(solution)/shard_map/reduce_scatter | solution.py:156
  66.3 0.5 copy-start.5
  67.2 6.6 %copy-start.9 = (u32[128]{0:T(128)S(1)}, u32[128]{0:T(128)}, u32[]{:S(2)}) copy-start(u32[128]{0:T(128)} %constant.46) | copy-start | bytes 1540
  67.2 7.9 %copy-start.7 = (s32[32]{0:T(128)S(1)}, s32[32]{0:T(128)}, u32[]{:S(2)}) copy-start(s32[32]{0:T(128)} %param.21) | copy-start | bytes 388
  67.2 293.3 %copy-start.3 = (bf16[32,1152]{1,0:T(8,128)(2,1)S(1)}, bf16[32,1152]{1,0:T(8,128)(2,1)}, u32[]{:S(2)}) copy-start(bf16[32,1152]{1,0:T(8,128)(2,1)} %param.20) | copy-start | bytes 221188
  424.4 12.5 %copy-start.1 = (bf16[1152,1152]{0,1:T(8,128)(2,1)S(1)}, bf16[1152,1152]{0,1:T(8,128)(2,1)}, u32[]{:S(2)}) copy-start(bf16[1152,1152]{0,1:T(8,128)(2,1)} %copy.67) | copy-start | bytes 7962628
  452.2 5.4 copy-start.2
  457.6 2.5 copy-start.6
  457.6 2.5 copy-start.8
Sparse Core Ops, SparseCore 0:
  461.7 68.1 reduce-scatter.1
where the time goes:
time: 540 us; the launch traced here: 538 us
  blocking collectives  321 us (59%)
  waiting for transfers between devices  71.9 us (13%)
  local copies, waits for them, and re-layouts  53.1 us (10%)
  matrix products  48.5 us (9%)
  between operations  16.3 us (3%)
  starting transfers between devices  15.8 us (3%)
  other arithmetic  12.2 us (2%)
    unnamed x1, blocking collectives  285 us
    reduce_scatter x1, waiting for transfers between devices, per_device(): lax.psum_scatter(text_term.astype(jnp.bfloat16), 'loop', scatter_dimensio...  67.5 us
    all_gather x1, blocking collectives, per_device(): text_block = lax.all_gather(text_unit, 'loop', axis=0, tiled=True)  35.4 us
    scatter x1, local copies, waits for them, and re-layouts, per_device(): send_tokens = jnp.zeros((slot_count, crop_width, model_width), jnp.bfloat...  23.5 us
    dot_general x2, matrix products, crop_partial(): jnp.einsum('...kh,...kd->...hd', weight, tokens.astype(jnp.float32), prec...  16.9 us
    dot_general x2, matrix products, crop_partial(): jnp.dot(flat_rows, key_probe, preferred_element_type=jnp.float32)  14.5 us
    dot_general x2, matrix products, crop_partial(): jnp.einsum('...hd,dhe->...he', mixed, value_heads, precision=highest)  12.3 us
  transfers between devices with their start and end apart: 4, of which 2 were waited for; matrix products, arithmetic and copies ran while one was open for 9% of the time, Pallas kernels for 0%

commit v1 on v0

--- a/solution.py
+++ b/solution.py
@@ -148,7 +148,8 @@
     text_unit = unit_rows(text_embed.astype(jnp.float32))
     scale_value = logit_scale[0]
     bias_value = logit_bias[0]
-    text_block = lax.all_gather(text_unit, "loop", axis=0, tiled=True)
+    sent = jnp.stack([text_unit] * lax.axis_size("loop"))
+    text_block = jnp.concatenate(lax.all_to_all(sent, "loop", 0, 0), axis=0)
     block_labels = lax.all_gather(pair_labels, "loop", axis=0, tiled=True)
     image_term, text_term = tile_terms(
         image_unit, text_block, block_labels, pair_labels, scale_value, bias_value

time: 540 us -> 512 us (0.948)
  blocking collectives: 321 us -> 285 us
    all_gather x1 -> x0, blocking collectives: 35.4 us -> none  [per_device(): text_block = lax.all_gather(text_unit, 'loop', axis=0, tiled=True)]
  transfers between devices with their start and end apart: 4 -> 5, of which waited for: 2 -> 2; matrix products, arithmetic and copies ran while one was open for 9% -> 21% of each run, Pallas kernels for 0% -> 0%
where the time goes in v1:
time: 512 us; the launch traced here: 511 us
  blocking collectives  285 us (56%)
  waiting for transfers between devices  74.5 us (15%)
  local copies, waits for them, and re-layouts  53.7 us (10%)
  matrix products  48.5 us (9%)
  starting transfers between devices  20.7 us (4%)
  between operations  16.2 us (3%)
  other arithmetic  12.3 us (2%)
    unnamed x1, blocking collectives  285 us
    reduce_scatter x1, waiting for transfers between devices, per_device(): lax.psum_scatter(text_term.astype(jnp.bfloat16), 'loop', scatter_dimensio...  70.1 us
    scatter x1, local copies, waits for them, and re-layouts, per_device(): send_tokens = jnp.zeros((slot_count, crop_width, model_width), jnp.bfloat...  23.5 us
    dot_general x2, matrix products, crop_partial(): jnp.einsum('...kh,...kd->...hd', weight, tokens.astype(jnp.float32), prec...  16.9 us
    dot_general x2, matrix products, crop_partial(): jnp.dot(flat_rows, key_probe, preferred_element_type=jnp.float32)  14.5 us
    dot_general x2, matrix products, crop_partial(): jnp.einsum('...hd,dhe->...he', mixed, value_heads, precision=highest)  12.3 us
  transfers between devices with their start and end apart: 5, of which 2 were waited for; matrix products, arithmetic and copies ran while one was open for 21% of the time, Pallas kernels for 0%

profile of v1, /device:TPU:0, one launch (start us, length us, event | category | flops | bytes accessed | tf_op | source)
XLA Modules:
  0.0 510.8 jit_solution(8131910111657612544)
XLA Ops:
  7.2 0.9 fusion.41
  8.2 0.8 select_reduce_fusion.1
  9.0 0.7 fusion.48
  9.7 0.9 scatter_custom_fusion.1
  10.6 0.7 all_to_all.20
  11.3 6.5 %all-to-all-start.1 = ((s32[16,1,8]{2,1,0:T(1,128)}), s32[16,1,8]{2,1,0:T(1,128)S(1)}, u32[]{:S(2)}, u32[]{:S(2)}) async-start(s32[16,1,8]{2,1,0:T(1,128)} %bitcast.8), calls=%async_computation.1 | async-start | bytes 16384 | tf_op jit(solution)/shard_map/all_to_all | solution.py:128
  17.7 0.9 scatter_custom_fusion
  18.6 0.7 all_to_all.18
  19.3 4.4 all-to-all-done.1
  23.7 3.5 all-to-all-start
  27.2 7.2 %broadcast_in_dim.92 = bf16[128,64,1152]{2,1,0:T(8,128)(2,1)} broadcast(bf16[]{:T(256)} %constant.10.clone.1), dimensions={} | broadcast | bytes 18874370 | tf_op jit(solution)/shard_map/broadcast_in_dim | solution.py:116
  34.4 23.5 %scatter_fusion = bf16[128,64,1152]{2,1,0:T(8,128)(2,1)} fusion(bf16[128,64,1152]{2,1,0:T(8,128)(2,1)} %broadcast_in_dim.92, s32[64]{0:T(128)S(1)} %fusion.48, bf16[64,64,1152]{2,1,0:T(8,128)(2,1)} %param.12), kind=kCustom, calls=%fused_computation.2 | custom fusion | bytes 28311808 | tf_op jit(solution)/shard_map/scatter | solution.py:118
  57.9 5.8 %all-to-all-start.2 = ((bf16[16,8,64,1152]{3,2,1,0:T(8,128)(2,1)}), bf16[16,8,64,1152]{3,2,1,0:T(8,128)(2,1)}, u32[]{:S(2)}, u32[]{:S(2)}) async-start(bf16[16,8,64,1152]{3,2,1,0:T(8,128)(2,1)} %bitcast.61), calls=%async_computation.2 | async-start | bytes 37748736 | tf_op jit(solution)/shard_map/all_to_all | solution.py:121
  63.7 2.4 convolution_multiply_fusion.1
  66.2 0.3 fusion.32
  66.6 0.3 fusion.33
  66.9 5.3 %copy.67 = bf16[1152,1152]{0,1:T(8,128)(2,1)} copy(bf16[1152,1152]{1,0:T(8,128)(2,1)} %param.18) | data formatting | bytes 5308416 | tf_op args[6]
  73.6 0.6 dynamic-slice
  74.8 0.2 dynamic-update-slice
  75.1 284.8 %all-reduce = s32[256]{0:T(256)S(1)} all-reduce(s32[256]{0:T(256)S(1)} %dynamic-update-slice), channel_id=1, replica_groups=mesh['dp'=16,'loop'=8] {'loop'}, use_global_device_ids=true, to_apply=%add | all-reduce | flops 256 | bytes 2048
  360.0 4.4 fusion.34
  364.6 0.5 broadcast.94
  365.1 0.7 reduce.3
  366.0 0.9 stack.2
  366.8 4.7 all-to-all-start.3
  371.6 0.2 reduce-scatter.2.cloned.1.call-start
  371.8 12.1 %convolution_multiply_fusion = f32[8192,16]{0,1:T(8,128)} fusion(bf16[8192,1152]{1,0:T(8,128)(2,1)} %bitcast.11, bf16[1152,16]{0,1:T(8,128)(2,1)S(1)} %copy-done.4), kind=kOutput, calls=%fused_computation.5 | convolution fusion | flops 302120960 | bytes 19435520 | tf_op jit(solution)/shard_map/dot_general | solution.py:19
  383.9 2.4 reshape.124
  386.4 2.0 fusion.25
  388.4 0.2 select_reduce_fusion
  388.8 2.4 fusion.26
  391.3 0.9 mul.78
  392.2 2.1 copy.81
  394.3 12.4 %fusion.27 = f32[16,8,16,1152]{3,2,1,0:T(8,128)S(1)} fusion(bf16[16,8,64,1152]{3,2,1,0:T(8,128)(2,1)} %all-to-all-done.2, f32[16,8,64,16]{2,1,0,3:T(8,128)} %reshape.124, f32[16,8,16]{2,1,0:T(8,128)S(1)} %fusion.25, pred[16,8,64]{2,1,0:T(8,128)(4,1)S(1)} %iota_compare_fusion), kind=kOutput, calls=%fused_computation.33 | convolution fusion | flops 1812332544 | bytes 28852224 | tf_op jit(solution)/shard_map/...kh,...kd->...hd/dot_general | solution.py:27
  406.7 7.0 %fusion.4 = f32[16,8,16,72]{3,1,0,2:T(8,128)S(1)} fusion(bf16[1152,16,72,1]{0,2,3,1:T(8,128)(2,1)S(1)} %bitcast.63, f32[16,8,16,1152]{3,2,1,0:T(8,128)S(1)} %fusion.27), kind=kOutput, calls=%fused_computation.9 | convolution fusion | flops 2038431744 | bytes 12681216 | tf_op jit(solution)/shard_map/...hd,dhe->...he/dot_general | solution.py:29
  413.7 1.6 copy.79
  415.3 2.5 reshape_reshape_reshape.3
  417.8 2.1 multiply_bitcast_fusion
  419.9 2.1 copy.82
  422.1 5.3 %fusion.10 = f32[32,16,72]{2,0,1:T(8,128)S(1)} fusion(bf16[1152,16,72]{0,2,1:T(8,128)(2,1)} %bitcast.62, f32[32,16,1152]{2,1,0:T(8,128)} %fusion.34, f32[32,16]{0,1:T(8,128)S(1)} %subtract_exponential_fusion), kind=kOutput, calls=%fused_computation.11 | convolution fusion | flops 509644800 | bytes 5163008 | tf_op jit(solution)/shard_map/...hd,dhe->...he/dot_general | solution.py:29
  427.4 0.9 fusion.14
  428.4 0.2 convert_element_type.37
  428.5 1.3 multiply_reduce_fusion
  429.9 0.3 fusion.23
  430.2 1.2 convolution_convert_fusion
  431.4 0.9 fusion.57
  432.3 70.1 %reduce-scatter.2.cloned.1.call-done = bf16[32,1152]{1,0:T(8,128)(2,1)} async-done(((bf16[256,1152]{1,0:T(8,128)(2,1)}), bf16[32,1152]{1,0:T(8,128)(2,1)}) %reduce-scatter.2.cloned.1.call-update) | async-done | bytes 73744 | tf_op jit(solution)/shard_map/reduce_scatter | solution.py:157
  502.4 1.6 convert_element_type.44
  (38 shorter events, 1.3 us)
Async XLA Ops:
  7.2 421.4 %copy-start = (bf16[1152,1152]{1,0:T(8,128)(2,1)S(1)}, bf16[1152,1152]{1,0:T(8,128)(2,1)}, u32[]{:S(2)}) copy-start(bf16[1152,1152]{1,0:T(8,128)(2,1)} %param.19) | copy-start | bytes 7962628
  11.3 12.5 %all-to-all-start.1 = ((s32[16,1,8]{2,1,0:T(1,128)}), s32[16,1,8]{2,1,0:T(1,128)S(1)}, u32[]{:S(2)}, u32[]{:S(2)}) async-start(s32[16,1,8]{2,1,0:T(1,128)} %bitcast.8), calls=%async_computation.1 | async-start | bytes 16384 | tf_op jit(solution)/shard_map/all_to_all | solution.py:128
  23.7 34.1 %all-to-all-start = ((s32[16,1,8]{2,1,0:T(1,128)}), s32[16,1,8]{2,1,0:T(1,128)S(1)}, u32[]{:S(2)}, u32[]{:S(2)}) async-start(s32[16,1,8]{2,1,0:T(1,128)} %bitcast.6), calls=%async_computation | async-start | bytes 16384 | tf_op jit(solution)/shard_map/all_to_all | solution.py:131
  57.9 5.8 %copy-start.4 = (bf16[1152,16]{0,1:T(8,128)(2,1)S(1)}, bf16[1152,16]{0,1:T(8,128)(2,1)}, u32[]{:S(2)}) copy-start(bf16[1152,16]{0,1:T(8,128)(2,1)} %param.17) | copy-start | bytes 110596
  57.9 308.1 %all-to-all-start.2 = ((bf16[16,8,64,1152]{3,2,1,0:T(8,128)(2,1)}), bf16[16,8,64,1152]{3,2,1,0:T(8,128)(2,1)}, u32[]{:S(2)}, u32[]{:S(2)}) async-start(bf16[16,8,64,1152]{3,2,1,0:T(8,128)(2,1)} %bitcast.61), calls=%async_computation.2 | async-start | bytes 37748736 | tf_op jit(solution)/shard_map/all_to_all | solution.py:121
  66.9 6.6 %copy-start.6 = (u32[128]{0:T(128)S(1)}, u32[128]{0:T(128)}, u32[]{:S(2)}) copy-start(u32[128]{0:T(128)} %constant.46) | copy-start | bytes 1540
  66.9 7.9 %copy-start.5 = (s32[32]{0:T(128)S(1)}, s32[32]{0:T(128)}, u32[]{:S(2)}) copy-start(s32[32]{0:T(128)} %param.21) | copy-start | bytes 388
  66.9 293.0 %copy-start.3 = (bf16[32,1152]{1,0:T(8,128)(2,1)S(1)}, bf16[32,1152]{1,0:T(8,128)(2,1)}, u32[]{:S(2)}) copy-start(bf16[32,1152]{1,0:T(8,128)(2,1)} %param.20) | copy-start | bytes 221188
  366.8 63.1 %all-to-all-start.3 = ((bf16[8,32,1152]{2,1,0:T(8,128)(2,1)}), bf16[8,32,1152]{2,1,0:T(8,128)(2,1)S(1)}, u32[]{:S(2)}, u32[]{:S(2)}) async-start(bf16[8,32,1152]{2,1,0:T(8,128)(2,1)} %stack.2), calls=%async_computation.3 | async-start | bytes 1179648 | tf_op jit(solution)/shard_map/all_to_all | solution.py:152
  371.6 130.8 %reduce-scatter.2.cloned.1.call-start = ((), (), s32[]{:S(2)}) async-start(), calls=%async_computation.5 | async-start | bytes 663552 | tf_op jit(solution)/shard_map/reduce_scatter | solution.py:157
  394.3 12.5 %copy-start.1 = (bf16[1152,1152]{0,1:T(8,128)(2,1)S(1)}, bf16[1152,1152]{0,1:T(8,128)(2,1)}, u32[]{:S(2)}) copy-start(bf16[1152,1152]{0,1:T(8,128)(2,1)} %copy.67) | copy-start | bytes 7962628
  422.1 5.3 %copy-start.2 = (f32[1152,128]{1,0:T(8,128)S(1)}, f32[1152,128]{1,0:T(8,128)}, u32[]{:S(2)}) copy-start(f32[1152,128]{1,0:T(8,128)} %copy.82) | copy-start | bytes 1769476
Sparse Core Ops, SparseCore 0:
  431.5 70.8 reduce-scatter.1
